TPU v7x, 32 devices: a whole 2x2x4 slice. The times are simulated.
32 devices in a mesh: ctx: 16 (over z, x, core), head: 2 (over y).
Axes of the slice: x: 2, y: 2, z: 4, core: 2. Of those that a mesh axis runs over, the one named last changes fastest.
Arguments:
- latent: bfloat16 [6144, 5120], P('ctx', 'head'), may hold values from -6 to 6
- probe: bfloat16 [6144, 5120], P('ctx'), may hold values from -6 to 6
- norm_gain: float32 [5120], replicated, may hold values from 0.25 to 1.75
- w_query: bfloat16 [5120, 3072], P('ctx', 'head'), may hold values from -2 to 2, as said below
- w_key: bfloat16 [5120, 3072], P('ctx', 'head'), may hold values from -2 to 2, as said below
- w_value: bfloat16 [5120, 3072], P('ctx', 'head'), may hold values from -0.078125 to 0.078125
- w_out: bfloat16 [3072, 5120], P('head', 'ctx'), may hold values from -0.109375 to 0.109375
- tile_mask: int32 [48, 48], replicated, may hold values from 0 to 1, as said below
Outputs:
- mixed: bfloat16 [6144, 5120], P('ctx', 'head')
- branch_tangent: bfloat16 [6144, 5120], P('ctx', 'head')
- trace_terms: float32 [6144], P('ctx')
Inputs may be any that keep to these rules, and one draw needn't show every extreme that they name: `tile_mask`: entry [q, k] is 0 where |q - k| > 3, and 1 where q == k or |q - k| == 3. `w_query`: entries of order 5120^-0.5. `w_key`: entries of order 5120^-0.5.
All inputs are finite; a program needn't handle non-finite values.
Results may differ from a plain program's by a relative error of at most 0.011.
Values may be sent and summed in bfloat16 or wider, within the bound.
A program may use at most 192 MiB of HBM per device.

v0:
```python
import jax
import jax.numpy as jnp
from jax import lax
from jax.sharding import PartitionSpec as P

D = 5120
HD = 128
TILE = 128


def with_halo(block, sides, width):
    for axis, dim in sides:
        count = lax.axis_size(axis)
        forward = [(i, i + 1) for i in range(count - 1)]
        backward = [(target, source) for source, target in forward]
        low = lax.ppermute(
            lax.slice_in_dim(block, block.shape[dim] - width, None, axis=dim), axis, forward
        )
        high = lax.ppermute(lax.slice_in_dim(block, 0, width, axis=dim), axis, backward)
        block = jnp.concatenate([low, block, high], axis=dim)
    return block


def attend_block(queries, queries_t, keys, values, keys_t, values_t, allowed):
    score_scale = HD ** (-0.5)
    scores = (
        jnp.einsum("qhd,khd->hqk", queries, keys, preferred_element_type=jnp.float32) * score_scale
    )
    masked = jnp.where(allowed[None], scores, -jnp.inf)
    highest = jnp.max(masked, -1, keepdims=True)
    expos = jnp.exp(masked - highest)
    probs = expos / jnp.sum(expos, -1, keepdims=True)
    scores_t = jnp.einsum("qhd,khd->hqk", queries_t, keys, preferred_element_type=jnp.float32)
    scores_t = (
        scores_t + jnp.einsum("qhd,khd->hqk", queries, keys_t, preferred_element_type=jnp.float32)
    ) * score_scale
    probs_t = probs * (scores_t - jnp.sum(probs * scores_t, -1, keepdims=True))
    probs_b = probs.astype(jnp.bfloat16)
    probs_tb = probs_t.astype(jnp.bfloat16)
    attended = jnp.einsum(
        "hqk,khd->qhd", probs_b, values, preferred_element_type=jnp.float32
    ).astype(jnp.bfloat16)
    attended_t = jnp.einsum("hqk,khd->qhd", probs_b, values_t, preferred_element_type=jnp.float32)
    attended_t = (
        attended_t
        + jnp.einsum("hqk,khd->qhd", probs_tb, values, preferred_element_type=jnp.float32)
    ).astype(jnp.bfloat16)
    return (attended, attended_t)


def shards(latent, probe, norm_gain, w_query, w_key, w_value, w_out, tile_mask):
    tok_rows, own_cols = latent.shape
    head_cols = w_query.shape[1]
    col_start = lax.axis_index("head") * own_cols
    tangent_own = lax.dynamic_slice_in_dim(probe, col_start, own_cols, 1).astype(jnp.float32)
    latent_f = latent.astype(jnp.float32)
    gain_own = lax.dynamic_slice_in_dim(norm_gain, col_start, own_cols, 0)
    squares, crossed = lax.psum(
        (jnp.sum(latent_f * latent_f, -1), jnp.sum(latent_f * tangent_own, -1)), "head"
    )
    inverse = lax.rsqrt(squares[:, None] / D + 1e-06)
    along = crossed[:, None] / D
    normed_own = (latent_f * inverse * gain_own).astype(jnp.bfloat16)
    normed_t_own = ((tangent_own * inverse - latent_f * inverse**3 * along) * gain_own).astype(
        jnp.bfloat16
    )
    normed, normed_t = (
        lax.all_gather(normed_own, "head", axis=1, tiled=True),
        lax.all_gather(normed_t_own, "head", axis=1, tiled=True),
    )

    def add_rows(weight_rows):
        first = jnp.dot(normed, weight_rows, preferred_element_type=jnp.float32)
        second = jnp.dot(normed_t, weight_rows, preferred_element_type=jnp.float32)
        return (first, second)

    pair_query = add_rows(lax.all_gather(w_query, "ctx", axis=0, tiled=True))
    pair_key = add_rows(lax.all_gather(w_key, "ctx", axis=0, tiled=True))
    pair_value = add_rows(lax.all_gather(w_value, "ctx", axis=0, tiled=True))
    heads_dev = head_cols // HD
    query = pair_query[0].astype(jnp.bfloat16).reshape(tok_rows, heads_dev, HD)
    query_t = pair_query[1].astype(jnp.bfloat16).reshape(tok_rows, heads_dev, HD)
    stacked = jnp.stack(
        [
            pair_key[0].astype(jnp.bfloat16),
            pair_value[0].astype(jnp.bfloat16),
            pair_key[1].astype(jnp.bfloat16),
            pair_value[1].astype(jnp.bfloat16),
        ]
    )
    beside_all = with_halo(stacked, (("ctx", 1),), tok_rows)
    beside_all = beside_all.reshape(4, 3 * tok_rows, heads_dev, HD)
    tiles_dev = tok_rows // TILE
    ctx_slot = lax.axis_index("ctx")
    mask_pad = jnp.pad(tile_mask, tiles_dev)
    tile_rows = lax.dynamic_slice(
        mask_pad,
        (ctx_slot * tiles_dev + tiles_dev, ctx_slot * tiles_dev),
        (tiles_dev, 3 * tiles_dev),
    )
    allowed = jnp.repeat(jnp.repeat(tile_rows, TILE, 0), TILE, 1) == 1
    attended, attended_t = attend_block(
        query, query_t, beside_all[0], beside_all[1], beside_all[2], beside_all[3], allowed
    )
    both_rows = jnp.concatenate(
        [attended.reshape(tok_rows, head_cols), attended_t.reshape(tok_rows, head_cols)], 0
    )
    terms = jnp.dot(
        both_rows,
        lax.all_gather(w_out, "ctx", axis=1, tiled=True),
        preferred_element_type=jnp.float32,
    )
    summed = lax.psum_scatter(
        terms.astype(jnp.bfloat16), "head", scatter_dimension=1, tiled=True
    ).astype(jnp.float32)
    branch = summed[:tok_rows]
    branch_t = summed[tok_rows:]
    mixed = (latent_f + branch).astype(jnp.bfloat16)
    trace_terms = lax.psum(jnp.sum(tangent_own * branch_t, -1), "head")
    return (mixed, branch_t.astype(jnp.bfloat16), trace_terms)


def solution(mesh):
    placed = (
        P("ctx", "head"),
        P("ctx", None),
        P(),
        P("ctx", "head"),
        P("ctx", "head"),
        P("ctx", "head"),
        P("head", "ctx"),
        P(),
    )
    return jax.shard_map(
        shards,
        mesh=mesh,
        in_specs=placed,
        out_specs=(P("ctx", "head"), P("ctx", "head"), P("ctx")),
        check_vma=False,
    )
```

profile of v0, /device:TPU:0, one launch (start us, length us, event | category | flops | bytes accessed | tf_op | source)
XLA Modules:
  0.0 851.1 jit_solution(12549174765315246761)
XLA Ops:
  7.2 0.9 dynamic_slice.9
  8.2 3.0 fusion.12
  11.1 5.9 all-reduce.1
  17.0 5.6 fusion.14
  22.7 0.7 all-gather.9.cloned.1.call-update
  23.4 0.7 all-gather.11.cloned.1.call-update
  24.2 0.5 all-gather.13.cloned.1.call-update
  24.7 0.5 all-gather.15.cloned.1.call-update
  25.3 0.5 all-gather.17.cloned.1.call-update
  26.1 52.3 %all-gather.7.cloned.1.call-done = bf16[384,5120]{1,0:T(8,128)(2,1)} async-done(((bf16[384,2560]{1,0:T(8,128)(2,1)}), bf16[384,5120]{1,0:T(8,128)(2,1)}) %all-gather.7.cloned.1.call-update) | async-done | bytes 3932176 | tf_op jit(solution)/shard_map/all_gather | solution.py:68
  78.4 122.6 %all-gather.9.cloned.1.call-done = bf16[5120,1536]{1,0:T(8,128)(2,1)} async-done(((bf16[320,1536]{1,0:T(8,128)(2,1)}), bf16[5120,1536]{1,0:T(8,128)(2,1)}) %all-gather.9.cloned.1.call-update) | async-done | bytes 15728656 | tf_op jit(solution)/shard_map/all_gather | solution.py:78
  201.0 10.8 %fusion.18 = bf16[1,384,1536]{2,1,0:T(8,128)(2,1)S(1)} fusion(bf16[384,5120]{1,0:T(8,128)(2,1)} %all-gather.7.cloned.1.call-done, bf16[5120,1536]{1,0:T(8,128)(2,1)} %all-gather.9.cloned.1.call-done), kind=kOutput, calls=%fused_computation.41 | convolution fusion | flops 6040387584 | bytes 20840448 | tf_op jit(solution)/shard_map/dot_general | solution.py:73
  211.8 110.0 %all-gather.11.cloned.1.call-done = bf16[5120,1536]{1,0:T(8,128)(2,1)} async-done(((bf16[320,1536]{1,0:T(8,128)(2,1)}), bf16[5120,1536]{1,0:T(8,128)(2,1)}) %all-gather.11.cloned.1.call-update) | async-done | bytes 15728656 | tf_op jit(solution)/shard_map/all_gather | solution.py:79
  321.8 10.8 %fusion.19 = bf16[1,384,1536]{2,1,0:T(8,128)(2,1)S(1)} fusion(bf16[384,5120]{1,0:T(8,128)(2,1)} %all-gather.7.cloned.1.call-done, bf16[5120,1536]{1,0:T(8,128)(2,1)} %all-gather.11.cloned.1.call-done), kind=kOutput, calls=%fused_computation.42 | convolution fusion | flops 6040387584 | bytes 20840448 | tf_op jit(solution)/shard_map/dot_general | solution.py:73
  332.6 43.2 %all-gather.13.cloned.1.call-done = bf16[384,5120]{1,0:T(8,128)(2,1)} async-done(((bf16[384,2560]{1,0:T(8,128)(2,1)}), bf16[384,5120]{1,0:T(8,128)(2,1)}) %all-gather.13.cloned.1.call-update) | async-done | bytes 3932176 | tf_op jit(solution)/shard_map/all_gather | solution.py:69
  375.8 10.9 %fusion.20 = bf16[1,384,1536]{2,1,0:T(8,128)(2,1)S(1)} fusion(bf16[384,5120]{1,0:T(8,128)(2,1)} %all-gather.13.cloned.1.call-done, bf16[5120,1536]{1,0:T(8,128)(2,1)} %all-gather.9.cloned.1.call-done), kind=kOutput, calls=%fused_computation.43 | convolution fusion | flops 6040387584 | bytes 20840448 | tf_op jit(solution)/shard_map/dot_general | solution.py:74
  386.7 0.8 copy-done.5
  387.5 1.4 copy-done.6
  389.0 6.2 fusion.21
  395.2 2.6 pad_maximum_fusion.1
  397.8 3.7 collective-permute-start
  401.5 1.5 collective-permute-start.1
  403.0 0.8 fusion.30
  404.0 0.9 broadcast_in_dim.17
  404.9 2.3 copy.22
  407.3 155.1 %all-gather.15.cloned.1.call-done = bf16[5120,1536]{1,0:T(8,128)(2,1)} async-done(((bf16[320,1536]{1,0:T(8,128)(2,1)}), bf16[5120,1536]{1,0:T(8,128)(2,1)}) %all-gather.15.cloned.1.call-update) | async-done | bytes 15728656 | tf_op jit(solution)/shard_map/all_gather | solution.py:77
  562.3 11.6 %convolution_convert_fusion.2 = bf16[384,1536]{1,0:T(8,128)(2,1)} fusion(bf16[384,5120]{1,0:T(8,128)(2,1)} %all-gather.7.cloned.1.call-done, bf16[5120,1536]{1,0:T(8,128)(2,1)} %all-gather.15.cloned.1.call-done), kind=kOutput, calls=%fused_computation.36 | convolution fusion | flops 6040387584 | bytes 20840448 | tf_op jit(solution)/shard_map/dot_general | solution.py:73
  573.9 2.4 copy.23
  576.3 11.6 %convolution_convert_fusion.1 = bf16[384,1536]{1,0:T(8,128)(2,1)} fusion(bf16[384,5120]{1,0:T(8,128)(2,1)} %all-gather.13.cloned.1.call-done, bf16[5120,1536]{1,0:T(8,128)(2,1)} %all-gather.15.cloned.1.call-done), kind=kOutput, calls=%fused_computation.35 | convolution fusion | flops 6040387584 | bytes 20840448 | tf_op jit(solution)/shard_map/dot_general | solution.py:74
  587.9 2.4 copy.28
  590.3 5.9 pad_maximum_fusion
  596.3 5.1 fusion.35
  601.3 4.4 copy.24
  605.7 5.8 copy.20
  611.5 6.1 copy.31
  617.6 5.8 copy.27
  623.4 13.7 %exponential_reduce_fusion = (f32[12,384]{1,0:T(8,128)}, f32[12,384,1152]{2,1,0:T(8,128)}) fusion(bf16[384,12,128]{0,2,1:T(8,128)(2,1)} %bitcast.66, bf16[1152,12,128]{0,2,1:T(8,128)(2,1)S(1)} %bitcast.55, pred[384,1152]{1,0:T(8,128)(4,1)} %copy.22), kind=kOutput, calls=%fused_computation.7 | convolution fusion | flops 1380189312 | bytes 26413056 | tf_op jit(solution)/shard_map/sub | solution.py:31
  637.0 12.8 %fusion.27 = bf16[12,128,384]{2,1,0:T(8,128)(2,1)} fusion(bf16[1152,12,128]{0,2,1:T(8,128)(2,1)} %bitcast.62, f32[12,384]{1,0:T(8,128)} %get-tuple-element.17, bf16[384,12,128]{0,2,1:T(8,128)(2,1)} %bitcast.67, bf16[1152,12,128]{0,2,1:T(8,128)(2,1)S(1)} %bitcast.56, pred[384,1152]{1,0:T(8,128)(4,1)} %copy.22), kind=kOutput, calls=%fused_computation.49 | convolution fusion | flops 2745046528 | bytes 9897984 | tf_op jit(solution)/shard_map/hqk,khd->qhd/dot_general | solution.py:40
  649.9 12.0 %fusion.36 = f32[12,384,1152]{2,1,0:T(8,128)} fusion(bf16[384,12,128]{0,2,1:T(8,128)(2,1)} %bitcast.60, bf16[1152,12,128]{0,2,1:T(8,128)(2,1)S(1)} %bitcast.57), kind=kOutput, calls=%fused_computation.61 | convolution fusion | flops 1358954496 | bytes 25952256 | tf_op jit(solution)/shard_map/qhd,khd->hqk/dot_general | solution.py:33
  661.8 25.8 %multiply_reduce_fusion = (f32[12,384]{1,0:T(8,128)}, f32[12,384,1152]{2,1,0:T(8,128)}) fusion(f32[12,384]{1,0:T(8,128)S(1)} %copy-done.7, f32[12,384,1152]{2,1,0:T(8,128)} %get-tuple-element.18, f32[12,384,1152]{2,1,0:T(8,128)} %fusion.36, bf16[384,12,128]{0,2,1:T(8,128)(2,1)S(1)} %bitcast.70, bf16[1152,12,128]{0,2,1:T(8,128)(2,1)} %bitcast.64), kind=kOutput, calls=%fused_computation.3 | convolution fusion | flops 1385491968 | bytes 68456448 | tf_op jit(solution)/shard_map/qhd,khd->hqk/dot_general | solution.py:35
  687.6 17.3 %fusion.2 = f32[12,128,384]{2,1,0:T(8,128)} fusion(bf16[1152,12,128]{0,2,1:T(8,128)(2,1)} %bitcast.63, f32[12,384,1152]{2,1,0:T(8,128)} %get-tuple-element.20, f32[12,384]{1,0:T(8,128)} %get-tuple-element.19, f32[12,384]{1,0:T(8,128)} %get-tuple-element.17, bf16[384,12,128]{0,2,1:T(8,128)(2,1)} %bitcast.68, bf16[1152,12,128]{0,2,1:T(8,128)(2,1)S(1)} %bitcast.58, ...), kind=kOutput, calls=%fused_computation.9 | convolution fusion | flops 2755073536 | bytes 32329728 | tf_op jit(solution)/shard_map/hqk,khd->qhd/dot_general | solution.py:46
  704.9 13.4 %add_convert_fusion = bf16[12,128,384]{2,1,0:T(8,128)(2,1)} fusion(f32[12,128,384]{2,1,0:T(8,128)} %fusion.2, bf16[1152,12,128]{0,2,1:T(8,128)(2,1)} %bitcast.61, f32[12,384]{1,0:T(8,128)} %get-tuple-element.17, bf16[384,12,128]{0,2,1:T(8,128)(2,1)} %bitcast.69, bf16[1152,12,128]{0,2,1:T(8,128)(2,1)S(1)} %bitcast.59, pred[384,1152]{1,0:T(8,128)(4,1)} %copy.22), kind=kOutput, calls=%fused_computation.48 | convolution fusion | flops 2745636352 | bytes 12257280 | tf_op jit(solution)/shard_map/hqk,khd->qhd/dot_general | solution.py:43
  718.3 18.4 %convolution_convert_fusion = bf16[768,5120]{1,0:T(8,128)(2,1)} fusion(bf16[1536,5120]{0,1:T(8,128)(2,1)} %all-gather.17.cloned.1.call-done, bf16[384,1536]{0,1:T(8,128)(2,1)} %bitcast.74, bf16[384,1536]{0,1:T(8,128)(2,1)} %bitcast.73), kind=kOutput, calls=%fused_computation.11 | convolution fusion | flops 12088246272 | bytes 25952256 | tf_op jit(solution)/shard_map/dot_general | solution.py:108
  736.8 93.2 %reduce-scatter.2.cloned.1.call-done = bf16[768,2560]{1,0:T(8,128)(2,1)} async-done(((bf16[768,5120]{1,0:T(8,128)(2,1)}), bf16[768,2560]{1,0:T(8,128)(2,1)}) %reduce-scatter.2.cloned.1.call-update) | async-done | bytes 3932176 | tf_op jit(solution)/shard_map/reduce_scatter | solution.py:113
  830.0 3.3 convert_element_type.77
  833.4 2.2 fusion.11
  835.6 5.5 psum.23
  841.0 2.9 slice.37
  (31 shorter events, 0.7 us)
Async XLA Ops:
  7.2 9.9 %copy-start = (bf16[384,2560]{1,0:T(8,128)(2,1)S(1)}, bf16[384,2560]{1,0:T(8,128)(2,1)}, u32[]{:S(2)}) copy-start(bf16[384,2560]{1,0:T(8,128)(2,1)} %param.8) | copy-start | bytes 5898244
  7.2 71.2 %all-gather.7.cloned.1.call-start = ((), (), s32[]{:S(2)}) async-start(), calls=%async_computation.1 | async-start | bytes 5898240 | tf_op jit(solution)/shard_map/all_gather | solution.py:68
  22.6 178.4 %all-gather.9.cloned.1.call-start = ((), (), s32[]{:S(2)}) async-start(), calls=%async_computation.2 | async-start | bytes 16711680 | tf_op jit(solution)/shard_map/all_gather | solution.py:78
  23.4 298.4 %all-gather.11.cloned.1.call-start = ((), (), s32[]{:S(2)}) async-start(), calls=%async_computation.3 | async-start | bytes 16711680 | tf_op jit(solution)/shard_map/all_gather | solution.py:79
  24.1 351.7 %all-gather.13.cloned.1.call-start = ((), (), s32[]{:S(2)}) async-start(), calls=%async_computation.4 | async-start | bytes 5898240 | tf_op jit(solution)/shard_map/all_gather | solution.py:69
  24.7 537.6 %all-gather.15.cloned.1.call-start = ((), (), s32[]{:S(2)}) async-start(), calls=%async_computation.5 | async-start | bytes 16711680 | tf_op jit(solution)/shard_map/all_gather | solution.py:77
  25.3 693.0 %all-gather.17.cloned.1.call-start = ((), (), s32[]{:S(2)}) async-start(), calls=%async_computation.6 | async-start | bytes 16711680 | tf_op jit(solution)/shard_map/all_gather | solution.py:110
  25.9 804.2 %reduce-scatter.2.cloned.1.call-start = ((), (), s32[]{:S(2)}) async-start(), calls=%async_computation.7 | async-start | bytes 11796480 | tf_op jit(solution)/shard_map/reduce_scatter | solution.py:113
  375.8 11.8 %copy-start.5 = (bf16[5120,1536]{1,0:T(8,128)(2,1)S(1)}, bf16[5120,1536]{1,0:T(8,128)(2,1)}, u32[]{:S(2)}) copy-start(bf16[5120,1536]{1,0:T(8,128)(2,1)} %all-gather.11.cloned.1.call-done) | copy-start | bytes 47185924
  375.8 13.2 %copy-start.6 = (bf16[384,5120]{1,0:T(8,128)(2,1)S(1)}, bf16[384,5120]{1,0:T(8,128)(2,1)}, u32[]{:S(2)}) copy-start(bf16[384,5120]{1,0:T(8,128)(2,1)} %all-gather.13.cloned.1.call-done) | copy-start | bytes 11796484
  395.2 2.6 copy-start.3
  397.8 192.6 %collective-permute-start = (bf16[4,384,1536]{2,1,0:T(8,128)(2,1)}, bf16[4,384,1536]{2,1,0:T(8,128)(2,1)}, u32[]{:S(2)}, u32[]{:S(2)}) collective-permute-start(bf16[4,384,1536]{2,1,0:T(8,128)(2,1)} %pad_maximum_fusion.1), channel_id=1, source_target_pairs={{0,2},{2,4},{4,6},{6,8},{8,10},{10,12},{12,14},{14,16},{16,18},{18... | collective-permute-start | bytes 14155784 | tf_op jit(solution)/shard_map/ppermute | solution.py:16
  401.5 188.8 %collective-permute-start.1 = (bf16[4,384,1536]{2,1,0:T(8,128)(2,1)}, bf16[4,384,1536]{2,1,0:T(8,128)(2,1)}, u32[]{:S(2)}, u32[]{:S(2)}) collective-permute-start(bf16[4,384,1536]{2,1,0:T(8,128)(2,1)} %pad_maximum_fusion.1), channel_id=1, source_target_pairs={{2,0},{4,2},{6,4},{8,6},{10,8},{12,10},{14,12},{16,14},{18,16},{20... | collective-permute-start | bytes 14155784 | tf_op jit(solution)/shard_map/ppermute | solution.py:19
  649.8 12.0 %copy-start.4 = (bf16[384,1536]{0,1:T(8,128)(2,1)S(1)}, bf16[384,1536]{0,1:T(8,128)(2,1)}, u32[]{:S(2)}) copy-start(bf16[384,1536]{0,1:T(8,128)(2,1)} %copy.23) | copy-start | bytes 3538948
  649.9 12.0 %copy-start.7 = (f32[12,384]{1,0:T(8,128)S(1)}, f32[12,384]{1,0:T(8,128)}, u32[]{:S(2)}) copy-start(f32[12,384]{1,0:T(8,128)} %get-tuple-element.17) | copy-start | bytes 55300
  736.8 96.6 %copy-start.1 = (bf16[384,2560]{1,0:T(8,128)(2,1)S(1)}, bf16[384,2560]{1,0:T(8,128)(2,1)}, u32[]{:S(2)}) copy-start(bf16[384,2560]{1,0:T(8,128)(2,1)} %param.8) | copy-start | bytes 5898244
  830.0 3.3 copy-start.2
Sparse Core Ops, SparseCore 0:
  22.8 55.5 all-gather.6
  80.7 120.2 all-gather.8
  203.3 118.4 all-gather.10
  323.8 51.9 all-gather.12
  377.9 184.3 all-gather.14
  564.5 119.2 all-gather.16
  736.9 93.0 reduce-scatter.1
where the time goes:
time: 855 us; the launch traced here: 851 us
  waiting for transfers between devices  579 us (68%)
  matrix products  175 us (20%)
  local copies, waits for them, and re-layouts  41.5 us (5%)
  other arithmetic  23.4 us (3%)
  between operations  14.5 us (2%)
  blocking collectives  11.3 us (1%)
    all_gather x1, waiting for transfers between devices, shards(): pair_query = add_rows(lax.all_gather(w_query, 'ctx', axis=0, tiled=True))  155 us
    all_gather x1, waiting for transfers between devices, shards(): pair_key = add_rows(lax.all_gather(w_key, 'ctx', axis=0, tiled=True))  123 us
    all_gather x1, waiting for transfers between devices, shards(): pair_value = add_rows(lax.all_gather(w_value, 'ctx', axis=0, tiled=True))  110 us
    reduce_scatter x1, waiting for transfers between devices, shards(): lax.psum_scatter(terms.astype(jnp.bfloat16), 'head', scatter_dimension=1,...  93.2 us
    all_gather x1, waiting for transfers between devices, shards(): lax.all_gather(normed_own, 'head', axis=1, tiled=True)  52.3 us
    all_gather x1, waiting for transfers between devices, shards(): lax.all_gather(normed_t_own, 'head', axis=1, tiled=True)  43.2 us
    dot_general x3, matrix products, add_rows(): first = jnp.dot(normed, weight_rows, preferred_element_type=jnp.float32)  33.2 us
    dot_general x3, matrix products, add_rows(): second = jnp.dot(normed_t, weight_rows, preferred_element_type=jnp.float32)  28.8 us
  transfers between devices with their start and end apart: 9, of which 6 were waited for; matrix products, arithmetic and copies ran while one was open for 24% of the time, Pallas kernels for 0%

commit v1 on v0

v1 whole, which is shorter than its diff:
```python
import functools

import jax
import jax.numpy as jnp
from jax import lax
from jax.experimental import pallas as pl
from jax.experimental.pallas import tpu as pltpu
from jax.sharding import PartitionSpec as P

D = 5120
HD = 128
TILE = 128
MESH = pl.DeviceIdType.MESH
MIB = 1 << 20


def chip_of(pos, chips):
    half = pos // (chips // 2)
    return (1 - half) * 2 * pos + half * (2 * (chips - 1 - pos) + 1)


def project_kernel(
    n, heads, lat_ref, probe_ref, gain_ref, w_ref,
    qkv_ref, wo_ref, proj_ref, halo_ref,
    lat_all, x_ref, wbuf, obuf,
    local_sem, ring_send, ring_recv, flip_send, flip_recv, own_send, own_recv,
    lat_send, lat_recv, lat_local, load_sem, store_sem, halo_send, halo_recv, halo_local,
):
    chips = n // 2
    hops = chips - 1
    tok, own = lat_ref.shape
    cols = proj_ref.shape[-1]
    width = wbuf.shape[-1]
    pieces = cols // width
    me = lax.axis_index("ctx")
    head = lax.axis_index("head")
    core = me % 2
    chip = me // 2
    cx = chip % 2
    cz = chip // 2
    pos = (1 - cx) * cz + cx * (chips - 1 - cz)
    ahead = chip_of((pos + 1) % chips, chips) * 2 + core
    behind = chip_of((pos + chips - 1) % chips, chips) * 2 + core
    twin = me + 1 - 2 * core
    right = (me + 1) % n
    left = (me + n - 1) % n

    barrier = pltpu.get_barrier_semaphore()
    for other in (ahead, behind, twin, right, left):
        pl.semaphore_signal(barrier, inc=1, device_id={"ctx": other}, device_id_type=MESH)
    for k in range(1, heads):
        pl.semaphore_signal(
            barrier, inc=1, device_id={"head": (head + k) % heads}, device_id_type=MESH
        )

    def full(w):
        return wo_ref if w == 3 else qkv_ref.at[w]

    def local_copy(w):
        return pltpu.make_async_copy(w_ref.at[w], full(w).at[me], local_sem.at[w])

    for w in range(4):
        local_copy(w).start()
    mine = pltpu.make_async_copy(lat_ref, lat_all.at[head], lat_local)
    mine.start()
    pl.semaphore_wait(barrier, 5 + heads - 1)

    def ring(w, hop, way):
        source = (pos + chips - hop) % chips if way == 0 else (pos + hop) % chips
        owner = chip_of(source, chips) * 2 + core
        block = full(w).at[owner, way]
        return pltpu.make_async_remote_copy(
            src_ref=block, dst_ref=block,
            send_sem=ring_send.at[w, hop, way], recv_sem=ring_recv.at[w, hop, way],
            device_id={"ctx": ahead if way == 0 else behind}, device_id_type=MESH,
        )

    def arrived(w, hop, way):
        source = (pos + chips - hop - 1) % chips if way == 0 else (pos + hop + 1) % chips
        return full(w).at[chip_of(source, chips) * 2 + core, way]

    def ring_wait(w, hop, way):
        block = arrived(w, hop, way)
        pltpu.make_async_remote_copy(
            src_ref=block, dst_ref=block,
            send_sem=ring_send.at[w, hop, way], recv_sem=ring_recv.at[w, hop, way],
            device_id={"ctx": ahead if way == 0 else behind}, device_id_type=MESH,
        ).wait_recv()

    def flip(w, hop, way):
        block = arrived(w, hop, way)
        return pltpu.make_async_remote_copy(
            src_ref=block, dst_ref=block,
            send_sem=flip_send.at[w, hop, way], recv_sem=flip_recv.at[w, hop, way],
            device_id={"ctx": twin}, device_id_type=MESH,
        )

    def flip_wait(w, hop, way):
        source = (pos + chips - hop - 1) % chips if way == 0 else (pos + hop + 1) % chips
        block = full(w).at[chip_of(source, chips) * 2 + 1 - core, way]
        pltpu.make_async_remote_copy(
            src_ref=block, dst_ref=block,
            send_sem=flip_send.at[w, hop, way], recv_sem=flip_recv.at[w, hop, way],
            device_id={"ctx": twin}, device_id_type=MESH,
        ).wait_recv()

    def own_flip(w, who):
        block = full(w).at[who]
        return pltpu.make_async_remote_copy(
            src_ref=block, dst_ref=block,
            send_sem=own_send.at[w], recv_sem=own_recv.at[w],
            device_id={"ctx": twin}, device_id_type=MESH,
        )

    def begin(w):
        ring(w, 0, 0).start()
        ring(w, 0, 1).start()
        own_flip(w, me).start()

    def advance(w, hop):
        for way in range(2):
            ring_wait(w, hop - 1, way)
            ring(w, hop, way).start()
            flip(w, hop - 1, way).start()

    def finish(w):
        for way in range(2):
            ring_wait(w, hops - 1, way)
            flip(w, hops - 1, way).start()

    def settle(w):
        own_flip(w, twin).wait_recv()

        @pl.loop(0, hops)
        def _(hop):
            for way in range(2):
                flip_wait(w, hop, way)

    def drain(w):
        own_flip(w, me).wait_send()

        @pl.loop(0, hops)
        def _(hop):
            for way in range(2):
                ring(w, hop, way).wait_send()
                flip(w, hop, way).wait_send()

    def lat_copy(k):
        return pltpu.make_async_remote_copy(
            src_ref=lat_ref, dst_ref=lat_all.at[head],
            send_sem=lat_send.at[k - 1], recv_sem=lat_recv.at[k - 1],
            device_id={"head": (head + k) % heads}, device_id_type=MESH,
        )

    def norm():
        mine.wait()
        for k in range(1, heads):
            came = lat_all.at[(head + heads - k) % heads]
            pltpu.make_async_remote_copy(
                src_ref=lat_ref, dst_ref=came,
                send_sem=lat_send.at[k - 1], recv_sem=lat_recv.at[k - 1],
                device_id={"head": (head + k) % heads}, device_id_type=MESH,
            ).wait_recv()
        step = 16

        @pl.loop(0, tok // step)
        def _(i):
            rows = pl.ds(pl.multiple_of(i * step, step), step)
            squares = jnp.zeros((step, 1), jnp.float32)
            crossed = jnp.zeros((step, 1), jnp.float32)
            for h in range(heads):
                part = lat_all[h, rows, :].astype(jnp.float32)
                tang = probe_ref[rows, h * own:(h + 1) * own].astype(jnp.float32)
                squares = squares + jnp.sum(part * part, -1, keepdims=True)
                crossed = crossed + jnp.sum(part * tang, -1, keepdims=True)
            inverse = lax.rsqrt(squares / D + 1e-06)
            along = crossed / D
            second = inverse * inverse * inverse * along
            rows_t = pl.ds(pl.multiple_of(tok + i * step, step), step)
            for h in range(heads):
                part = lat_all[h, rows, :].astype(jnp.float32)
                tang = probe_ref[rows, h * own:(h + 1) * own].astype(jnp.float32)
                gain = gain_ref[:, h * own:(h + 1) * own]
                x_ref[rows, h * own:(h + 1) * own] = (part * inverse * gain).astype(jnp.bfloat16)
                x_ref[rows_t, h * own:(h + 1) * own] = (
                    (tang * inverse - part * second) * gain
                ).astype(jnp.bfloat16)

    def load(w, piece, slot):
        at = pl.ds(pl.multiple_of(piece * width, width), width)
        return pltpu.make_async_copy(
            qkv_ref.at[w, :, :, :, at], wbuf.at[slot], load_sem.at[slot]
        )

    def multiply(w, piece, slot):
        load(w, piece, slot).wait()
        weight = wbuf[slot].reshape(D, width)
        rows = 128

        @pl.loop(0, 2 * tok // rows)
        def _(i):
            at = pl.ds(pl.multiple_of(i * rows, rows), rows)
            obuf[slot, at, :] = jnp.dot(
                x_ref[at, :], weight, preferred_element_type=jnp.float32
            ).astype(jnp.bfloat16)

        at = pl.ds(pl.multiple_of(piece * width, width), width)
        store = pltpu.make_async_copy(
            obuf.at[slot], proj_ref.at[w, :, at], store_sem.at[slot]
        )
        store.start()
        store.wait()

    def both(piece):
        load(0, piece, 0).start()
        load(1, piece, 1).start()
        multiply(0, piece, 0)
        multiply(1, piece, 1)

    def halo(side):
        return pltpu.make_async_remote_copy(
            src_ref=proj_ref.at[pl.ds(0, 2)], dst_ref=halo_ref.at[side],
            send_sem=halo_send.at[side], recv_sem=halo_recv.at[side],
            device_id={"ctx": right if side == 0 else left}, device_id_type=MESH,
        )

    def halo_fill(side):
        return pltpu.make_async_copy(
            proj_ref.at[pl.ds(0, 2)], halo_ref.at[side], halo_local
        )

    def halo_start():
        @pl.when(me < n - 1)
        def _():
            halo(0).start()

        @pl.when(me > 0)
        def _():
            halo(1).start()

        @pl.when(me == 0)
        def _():
            halo_fill(0).start()

        @pl.when(me == n - 1)
        def _():
            halo_fill(1).start()

    def halo_end():
        @pl.when(me < n - 1)
        def _():
            halo(0).wait_send()
            halo(1).wait_recv()

        @pl.when(me > 0)
        def _():
            halo(1).wait_send()
            halo(0).wait_recv()

        @pl.when(me == 0)
        def _():
            halo_fill(0).wait()

        @pl.when(me == n - 1)
        def _():
            halo_fill(1).wait()

    for w in range(4):
        local_copy(w).wait()
    begin(0)
    begin(1)
    for k in range(1, heads):
        lat_copy(k).start()

    @pl.loop(1, hops)
    def _(hop):
        advance(0, hop)
        advance(1, hop)

        @pl.when(hop == hops - 1)
        def _():
            norm()

    begin(2)
    begin(3)
    finish(0)
    finish(1)
    settle(0)
    settle(1)

    per = 3
    turns = -(-pieces // per)

    @pl.loop(1, hops)
    def _(hop):
        advance(2, hop)
        advance(3, hop)

        @pl.when(hop <= turns)
        def _():
            for j in range(per):
                piece = (hop - 1) * per + j
                if pieces % per:
                    pl.when(piece < pieces)(lambda piece=piece: both(piece))
                else:
                    both(piece)

        @pl.when(hop == turns + 1)
        def _():
            halo_start()

    finish(2)
    finish(3)
    settle(2)

    @pl.loop(0, pieces)
    def _(piece):
        load(2, piece, 0).start()
        multiply(2, piece, 0)

    settle(3)
    halo_end()
    for w in range(4):
        drain(w)
    for k in range(1, heads):
        lat_copy(k).wait_send()


def gather_and_project(latent, probe, gain, weights):
    n = lax.axis_size("ctx")
    heads = lax.axis_size("head")
    hops = n // 2 - 1
    tok, own = latent.shape
    rows, cols = weights.shape[1:]
    weights = weights.reshape(4, 2, rows // 2, cols)
    width = 256 if cols % 256 == 0 else 128
    dma = pltpu.SemaphoreType.DMA
    bf = jnp.bfloat16
    vmem = pl.BlockSpec(memory_space=pltpu.VMEM)
    anywhere = pl.BlockSpec(memory_space=pl.ANY)
    return pl.pallas_call(
        functools.partial(project_kernel, n, heads),
        out_shape=(
            jax.ShapeDtypeStruct((3, n, 2, rows // 2, cols), bf),
            jax.ShapeDtypeStruct((n, 2, rows // 2, cols), bf),
            jax.ShapeDtypeStruct((3, 2 * tok, cols), bf),
            jax.ShapeDtypeStruct((2, 2, 2 * tok, cols), bf),
        ),
        in_specs=[vmem, vmem, vmem, anywhere],
        out_specs=(anywhere,) * 4,
        scratch_shapes=[
            pltpu.VMEM((heads, tok, own), bf),
            pltpu.VMEM((2 * tok, D), bf),
            pltpu.VMEM((2, n, 2, rows // 2, width), bf),
            pltpu.VMEM((2, 2 * tok, width), bf),
            dma((4,)), dma((4, hops, 2)), dma((4, hops, 2)), dma((4, hops, 2)), dma((4, hops, 2)),
            dma((4,)), dma((4,)),
            dma((heads - 1,)), dma((heads - 1,)), dma, dma((2,)), dma((2,)),
            dma((2,)), dma((2,)), dma,
        ],
        compiler_params=pltpu.CompilerParams(
            collective_id=0, has_side_effects=True, vmem_limit_bytes=48 * MIB
        ),
    )(latent, probe, gain, weights)


def attend_kernel(tiles, mask_ref, q_ref, own_ref, low_ref, high_ref, out_ref, k_all, v_all):
    tok = tiles * TILE
    scale = HD ** (-0.5)
    for place, ref in enumerate((low_ref, own_ref, high_ref)):
        at = slice(place * tok, (place + 1) * tok)
        k_all[at, :HD] = ref[0, :tok, :]
        k_all[at, HD:] = ref[0, tok:, :]
        v_all[at, :HD] = ref[1, :tok, :]
        v_all[at, HD:] = ref[1, tok:, :]
    contract = (((1,), (1,)), ((), ()))
    band = 2 * tiles + 1
    for i in range(tiles):
        rows = slice(i * TILE, (i + 1) * TILE)
        rows_t = slice(tok + i * TILE, tok + (i + 1) * TILE)
        query = q_ref[0, rows, :]
        query_t = q_ref[0, rows_t, :]
        keys = k_all[i * TILE:(i + band) * TILE, :]
        scores = lax.dot_general(
            query, keys[:, :HD], contract, preferred_element_type=jnp.float32
        ) * scale
        scores_t = lax.dot_general(
            jnp.concatenate([query_t, query], 1), keys, contract,
            preferred_element_type=jnp.float32,
        ) * scale
        masked = jnp.concatenate(
            [
                jnp.where(
                    mask_ref[i, i + j] == 1, scores[:, j * TILE:(j + 1) * TILE], -1e30
                )
                for j in range(band)
            ],
            1,
        )
        highest = jnp.max(masked, -1, keepdims=True)
        expos = jnp.exp(masked - highest)
        probs = expos * (1.0 / jnp.sum(expos, -1, keepdims=True))
        weighed = probs * scores_t
        probs_t = weighed - probs * jnp.sum(weighed, -1, keepdims=True)
        probs_b = probs.astype(jnp.bfloat16)
        values = v_all[i * TILE:(i + band) * TILE, :]
        first = jnp.dot(probs_b, values, preferred_element_type=jnp.float32)
        second = first[:, HD:] + jnp.dot(
            probs_t.astype(jnp.bfloat16), values[:, :HD], preferred_element_type=jnp.float32
        )
        out_ref[rows, :] = first[:, :HD].astype(jnp.bfloat16)
        out_ref[rows_t, :] = second.astype(jnp.bfloat16)


def attend(tile_rows, proj, halo):
    rows, cols = proj.shape[1:]
    tok = rows // 2
    tiles = tok // TILE
    return pl.pallas_call(
        functools.partial(attend_kernel, tiles),
        grid=(cols // HD,),
        out_shape=jax.ShapeDtypeStruct((rows, cols), jnp.bfloat16),
        in_specs=[
            pl.BlockSpec(memory_space=pltpu.SMEM),
            pl.BlockSpec((1, rows, HD), lambda h: (2, 0, h)),
            pl.BlockSpec((2, rows, HD), lambda h: (0, 0, h)),
            pl.BlockSpec((None, 2, rows, HD), lambda h: (0, 0, 0, h)),
            pl.BlockSpec((None, 2, rows, HD), lambda h: (1, 0, 0, h)),
        ],
        out_specs=pl.BlockSpec((rows, HD), lambda h: (0, h)),
        scratch_shapes=[pltpu.VMEM((3 * tok, 2 * HD), jnp.bfloat16)] * 2,
        compiler_params=pltpu.CompilerParams(vmem_limit_bytes=32 * MIB),
    )(tile_rows, proj, proj, halo, halo)


def shards(latent, probe, norm_gain, w_query, w_key, w_value, w_out, tile_mask):
    tok_rows, own_cols = latent.shape
    weights = jnp.stack([w_key, w_value, w_query, w_out.T])
    _, wo_full, proj, halo = gather_and_project(latent, probe, norm_gain.reshape(1, D), weights)
    tiles_dev = tok_rows // TILE
    ctx_slot = lax.axis_index("ctx")
    mask_pad = jnp.pad(tile_mask, tiles_dev)
    tile_rows = lax.dynamic_slice(
        mask_pad,
        (ctx_slot * tiles_dev + tiles_dev, ctx_slot * tiles_dev),
        (tiles_dev, 3 * tiles_dev),
    )
    both_rows = attend(tile_rows, proj, halo)
    w_out_t = wo_full.reshape(D, w_out.shape[0])
    terms = lax.dot_general(
        both_rows, w_out_t, (((1,), (1,)), ((), ())), preferred_element_type=jnp.float32
    ).astype(jnp.bfloat16)
    summed = lax.psum_scatter(terms, "head", scatter_dimension=1, tiled=True).astype(jnp.float32)
    branch = summed[:tok_rows]
    branch_t = summed[tok_rows:]
    latent_f = latent.astype(jnp.float32)
    col_start = lax.axis_index("head") * own_cols
    tangent_own = lax.dynamic_slice_in_dim(probe, col_start, own_cols, 1).astype(jnp.float32)
    mixed = (latent_f + branch).astype(jnp.bfloat16)
    trace_terms = lax.psum(jnp.sum(tangent_own * branch_t, -1), "head")
    return (mixed, branch_t.astype(jnp.bfloat16), trace_terms)


def solution(mesh):
    placed = (
        P("ctx", "head"),
        P("ctx", None),
        P(),
        P("ctx", "head"),
        P("ctx", "head"),
        P("ctx", "head"),
        P("head", "ctx"),
        P(),
    )
    return jax.shard_map(
        shards,
        mesh=mesh,
        in_specs=placed,
        out_specs=(P("ctx", "head"), P("ctx", "head"), P("ctx")),
        check_vma=False,
    )
```

time: 855 us -> 756 us (0.88)
  Pallas kernels: 0 us -> 591 us
  waiting for transfers between devices: 579 us -> 106 us
  matrix products: 175 us -> 17.7 us
  local copies, waits for them, and re-layouts: 41.5 us -> 11.9 us
  other arithmetic: 23.4 us -> 9.39 us
    pallas_call x0 -> x2, Pallas kernels: none -> 591 us  [the longest x1 561 us: gather_and_project(): pl.pallas_call(functools.partial(project_kernel, n, heads), out_shape=(ja...]
    all_gather x6 -> x0, waiting for transfers between devices: 483 us -> none  [the longest x1 155 us: shards(): pair_query = add_rows(lax.all_gather(w_query, 'ctx', axis=0, tiled=True))]
    dot_general x12 -> x1, matrix products: 162 us -> 17.7 us  [shards(): lax.dot_general(both_rows, w_out_t, (((1,), (1,)), ((), ())), preferred_e...]
    slice x5 -> x0, local copies, waits for them, and re-layouts: 27.1 us -> none  [the longest x2 10.9 us: shards(): beside_all[3]]
    sub x1 -> x0, matrix products: 13.7 us -> none  [attend_block(): expos = jnp.exp(masked - highest)]
    reduce_scatter x1, waiting for transfers between devices: 93.2 us -> 106 us  [shards(): lax.psum_scatter(terms, 'head', scatter_dimension=1, tiled=True)]
  transfers between devices with their start and end apart: 9 -> 1, of which waited for: 6 -> 1; matrix products, arithmetic and copies ran while one was open for 24% -> 0% of each run, Pallas kernels for 0% -> 0%
where the time goes in v1:
time: 756 us; the launch traced here: 755 us
  Pallas kernels  591 us (78%)
  waiting for transfers between devices  106 us (14%)
  matrix products  17.7 us (2%)
  between operations  14.1 us (2%)
  local copies, waits for them, and re-layouts  11.9 us (2%)
  other arithmetic  9.39 us (1%)
    pallas_call x1, Pallas kernels, gather_and_project(): pl.pallas_call(functools.partial(project_kernel, n, heads), out_shape=(ja...  561 us
    reduce_scatter x1, waiting for transfers between devices, shards(): lax.psum_scatter(terms, 'head', scatter_dimension=1, tiled=True)  106 us
    pallas_call x1, Pallas kernels, attend(): pl.pallas_call(functools.partial(attend_kernel, tiles), grid=(cols // HD,...  29.2 us
    dot_general x1, matrix products, shards(): lax.dot_general(both_rows, w_out_t, (((1,), (1,)), ((), ())), preferred_e...  17.7 us
  transfers between devices with their start and end apart: 1, of which 1 were waited for; matrix products, arithmetic and copies ran while one was open for 0% of the time, Pallas kernels for 0%

profile of v1, /device:TPU:0, one launch (start us, length us, event | category | flops | bytes accessed | tf_op | source)
XLA Modules:
  0.0 755.0 jit_solution(5453743197928737512)
XLA Ops:
  7.2 0.0 reduce-scatter.2.cloned.1.call-start
  7.2 0.8 pad_dynamic-slice_fusion.mask_ref
  8.0 0.0 copy-start.2
  8.0 0.0 copy-start.4
  8.0 0.0 copy-start.5
  8.0 3.9 pad_maximum_fusion.w_ref
  11.9 0.6 copy-done.2
  12.5 0.9 copy-done.4
  13.4 0.0 copy-done.5
  13.4 561.5 %shard_map.103 = (bf16[3,16,2,160,1536]{4,3,2,1,0:T(8,128)(2,1)}, bf16[16,2,160,1536]{3,2,1,0:T(8,128)(2,1)}, bf16[3,768,1536]{2,1,0:T(8,128)(2,1)}, bf16[2,2,768,1536]{3,2,1,0:T(8,128)(2,1)}) custom-call(bf16[384,2560]{1,0:T(8,128)(2,1)S(1)} %copy-done.4, bf16[384,5120]{1,0:T(8,128)(2,1)S(1)} %copy-done.2, f32[1,5120]{1,0:T(1,128)S(1)} %bitcast.10, ...), custom_call_target="tpu_custom_call" | custom-call | tf_op jit(solution)/shard_map/pallas_call | solution.py:341
  574.8 0.0 copy-start
  574.8 3.7 copy-done
  578.5 0.0 copy-start.1
  578.5 3.0 copy-done.1
  581.5 29.2 %shard_map.104 = bf16[768,1536]{1,0:T(8,128)(2,1)S(1)} custom-call(s32[3,9]{1,0:T(4,128)S(1)} %pad_dynamic-slice_fusion.mask_ref, bf16[3,768,1536]{2,1,0:T(8,128)(2,1)S(1)} %copy-done.1, bf16[3,768,1536]{2,1,0:T(8,128)(2,1)S(1)} %copy-done.1, bf16[2,2,768,1536]{3,2,1,0:T(8,128)(2,1)S(1)} %copy-done, bf16[2,2,768,1536]{3,2,1,0:T(8,128)(2,1)S(1)} %copy-done), custom_call_target="tpu_custom_call" | custom-call | tf_op jit(solution)/shard_map/pallas_call | solution.py:419
  610.8 17.7 %convolution_convert_fusion = bf16[768,5120]{1,0:T(8,128)(2,1)} fusion(bf16[768,1536]{1,0:T(8,128)(2,1)S(1)} %shard_map.104, bf16[5120,1536]{1,0:T(8,128)(2,1)} %bitcast.15), kind=kOutput, calls=%fused_computation | convolution fusion | flops 12083527680 | bytes 25952256 | tf_op jit(solution)/shard_map/dot_general | solution.py:450
  628.5 0.0 reduce-scatter.2.cloned.1.call-update
  628.5 105.7 %reduce-scatter.2.cloned.1.call-done = bf16[768,2560]{1,0:T(8,128)(2,1)} async-done(((bf16[768,5120]{1,0:T(8,128)(2,1)}), bf16[768,2560]{1,0:T(8,128)(2,1)}) %reduce-scatter.2.cloned.1.call-update) | async-done | bytes 3932176 | tf_op jit(solution)/shard_map/reduce_scatter | solution.py:453
  734.2 0.0 copy-start.3
  734.2 3.3 convert_element_type.20
  737.5 0.0 copy-done.3
  737.5 2.2 multiply_reduce_fusion
  739.7 5.5 psum.7
  745.2 2.9 slice.15
Async XLA Ops:
  7.2 727.0 %reduce-scatter.2.cloned.1.call-start = ((), (), s32[]{:S(2)}) async-start(), calls=%async_computation.1 | async-start | bytes 11796480 | tf_op jit(solution)/shard_map/reduce_scatter | solution.py:453
  8.0 4.5 copy-start.2
  8.0 5.3 copy-start.4
  8.0 5.3 copy-start.5
  574.8 3.7 copy-start
  578.5 3.0 copy-start.1
  734.2 3.3 copy-start.3
Sparse Core Ops, SparseCore 0:
  628.7 105.4 reduce-scatter.1

commit v2 on v1

--- a/solution.py
+++ b/solution.py
@@ -65,12 +65,12 @@
     mine.start()
     pl.semaphore_wait(barrier, 5 + heads - 1)
 
-    def ring(w, hop, way):
+    def ring(w, hop, way, first=False):
         source = (pos + chips - hop) % chips if way == 0 else (pos + hop) % chips
         owner = chip_of(source, chips) * 2 + core
         block = full(w).at[owner, way]
         return pltpu.make_async_remote_copy(
-            src_ref=block, dst_ref=block,
+            src_ref=w_ref.at[w, way] if first else block, dst_ref=block,
             send_sem=ring_send.at[w, hop, way], recv_sem=ring_recv.at[w, hop, way],
             device_id={"ctx": ahead if way == 0 else behind}, device_id_type=MESH,
         )
@@ -105,16 +105,15 @@
         ).wait_recv()
 
     def own_flip(w, who):
-        block = full(w).at[who]
         return pltpu.make_async_remote_copy(
-            src_ref=block, dst_ref=block,
+            src_ref=w_ref.at[w], dst_ref=full(w).at[who],
             send_sem=own_send.at[w], recv_sem=own_recv.at[w],
             device_id={"ctx": twin}, device_id_type=MESH,
         )
 
     def begin(w):
-        ring(w, 0, 0).start()
-        ring(w, 0, 1).start()
+        ring(w, 0, 0, True).start()
+        ring(w, 0, 1, True).start()
         own_flip(w, me).start()
 
     def advance(w, hop):
@@ -129,6 +128,7 @@
             flip(w, hops - 1, way).start()
 
     def settle(w):
+        local_copy(w).wait()
         own_flip(w, twin).wait_recv()
 
         @pl.loop(0, hops)
@@ -211,62 +211,62 @@
         store.start()
         store.wait()
 
-    def both(piece):
-        load(0, piece, 0).start()
-        load(1, piece, 1).start()
-        multiply(0, piece, 0)
-        multiply(1, piece, 1)
-
-    def halo(side):
+    def fetch(q, slot):
+        @pl.when(q < 2 * pieces)
+        def _():
+            load(q // pieces, q % pieces, slot).start()
+
+    def work(q, slot):
+        @pl.when(q < 2 * pieces)
+        def _():
+            multiply(q // pieces, q % pieces, slot)
+
+    def halo(side, a):
         return pltpu.make_async_remote_copy(
-            src_ref=proj_ref.at[pl.ds(0, 2)], dst_ref=halo_ref.at[side],
-            send_sem=halo_send.at[side], recv_sem=halo_recv.at[side],
+            src_ref=proj_ref.at[a], dst_ref=halo_ref.at[side, a],
+            send_sem=halo_send.at[side, a], recv_sem=halo_recv.at[side, a],
             device_id={"ctx": right if side == 0 else left}, device_id_type=MESH,
         )
 
-    def halo_fill(side):
-        return pltpu.make_async_copy(
-            proj_ref.at[pl.ds(0, 2)], halo_ref.at[side], halo_local
-        )
-
-    def halo_start():
+    def halo_fill(side, a):
+        return pltpu.make_async_copy(proj_ref.at[a], halo_ref.at[side, a], halo_local.at[a])
+
+    def halo_start(a):
         @pl.when(me < n - 1)
         def _():
-            halo(0).start()
+            halo(0, a).start()
 
         @pl.when(me > 0)
         def _():
-            halo(1).start()
+            halo(1, a).start()
 
         @pl.when(me == 0)
         def _():
-            halo_fill(0).start()
+            halo_fill(0, a).start()
 
         @pl.when(me == n - 1)
         def _():
-            halo_fill(1).start()
-
-    def halo_end():
+            halo_fill(1, a).start()
+
+    def halo_end(a):
         @pl.when(me < n - 1)
         def _():
-            halo(0).wait_send()
-            halo(1).wait_recv()
+            halo(0, a).wait_send()
+            halo(1, a).wait_recv()
 
         @pl.when(me > 0)
         def _():
-            halo(1).wait_send()
-            halo(0).wait_recv()
+            halo(1, a).wait_send()
+            halo(0, a).wait_recv()
 
         @pl.when(me == 0)
         def _():
-            halo_fill(0).wait()
+            halo_fill(0, a).wait()
 
         @pl.when(me == n - 1)
         def _():
-            halo_fill(1).wait()
-
-    for w in range(4):
-        local_copy(w).wait()
+            halo_fill(1, a).wait()
+
     begin(0)
     begin(1)
     for k in range(1, heads):
@@ -288,38 +288,38 @@
     settle(0)
     settle(1)
 
-    per = 3
-    turns = -(-pieces // per)
-
     @pl.loop(1, hops)
     def _(hop):
+        q = (hop - 1) * 4
+        fetch(q, 0)
+        fetch(q + 1, 1)
         advance(2, hop)
+        work(q, 0)
+        fetch(q + 2, 0)
+        work(q + 1, 1)
+        fetch(q + 3, 1)
         advance(3, hop)
-
-        @pl.when(hop <= turns)
-        def _():
-            for j in range(per):
-                piece = (hop - 1) * per + j
-                if pieces % per:
-                    pl.when(piece < pieces)(lambda piece=piece: both(piece))
-                else:
-                    both(piece)
-
-        @pl.when(hop == turns + 1)
-        def _():
-            halo_start()
+        work(q + 2, 0)
+        work(q + 3, 1)
+        for a in range(2):
+
+            @pl.when(hop == -(-(a + 1) * pieces // 4))
+            def _(a=a):
+                halo_start(a)
 
     finish(2)
     finish(3)
     settle(2)
 
-    @pl.loop(0, pieces)
-    def _(piece):
-        load(2, piece, 0).start()
-        multiply(2, piece, 0)
+    load(2, 0, 0).start()
+    for piece in range(pieces):
+        if piece + 1 < pieces:
+            load(2, piece + 1, (piece + 1) % 2).start()
+        multiply(2, piece, piece % 2)
 
     settle(3)
-    halo_end()
+    halo_end(0)
+    halo_end(1)
     for w in range(4):
         drain(w)
     for k in range(1, heads):
@@ -356,7 +356,7 @@
             dma((4,)), dma((4, hops, 2)), dma((4, hops, 2)), dma((4, hops, 2)), dma((4, hops, 2)),
             dma((4,)), dma((4,)),
             dma((heads - 1,)), dma((heads - 1,)), dma, dma((2,)), dma((2,)),
-            dma((2,)), dma((2,)), dma,
+            dma((2, 2)), dma((2, 2)), dma((2,)),
         ],
         compiler_params=pltpu.CompilerParams(
             collective_id=0, has_side_effects=True, vmem_limit_bytes=48 * MIB

time: 756 us -> 611 us (0.81)
  Pallas kernels: 591 us -> 447 us
    pallas_call x1, Pallas kernels: 561 us -> 417 us  [gather_and_project(): pl.pallas_call(functools.partial(project_kernel, n, heads), out_shape=(ja...]
where the time goes in v2:
time: 611 us
  Pallas kernels  447 us (73%)
  waiting for transfers between devices  106 us (17%)
  matrix products  17.7 us (3%)
  between operations  14.1 us (2%)
  local copies, waits for them, and re-layouts  11.9 us (2%)
  other arithmetic  9.39 us (2%)
    pallas_call x1, Pallas kernels, gather_and_project(): pl.pallas_call(functools.partial(project_kernel, n, heads), out_shape=(ja...  417 us
    reduce_scatter x1, waiting for transfers between devices, shards(): lax.psum_scatter(terms, 'head', scatter_dimension=1, tiled=True)  106 us
    pallas_call x1, Pallas kernels, attend(): pl.pallas_call(functools.partial(attend_kernel, tiles), grid=(cols // HD,...  29.2 us
    dot_general x1, matrix products, shards(): lax.dot_general(both_rows, w_out_t, (((1,), (1,)), ((), ())), preferred_e...  17.7 us
  transfers between devices with their start and end apart: 1, of which 1 were waited for; matrix products, arithmetic and copies ran while one was open for 0% of the time, Pallas kernels for 0%

profile of v2, /device:TPU:0, one launch (start us, length us, event | category | flops | bytes accessed | tf_op | source)
XLA Modules:
  0.0 610.8 jit_solution(10204369535061117703)
XLA Ops:
  7.2 0.0 reduce-scatter.2.cloned.1.call-start
  7.2 0.8 pad_dynamic-slice_fusion.mask_ref
  8.0 0.0 copy-start.2
  8.0 0.0 copy-start.4
  8.0 0.0 copy-start.5
  8.0 3.9 pad_maximum_fusion.w_ref
  11.9 0.6 copy-done.2
  12.5 0.9 copy-done.4
  13.4 0.0 copy-done.5
  13.4 417.4 %shard_map.103 = (bf16[3,16,2,160,1536]{4,3,2,1,0:T(8,128)(2,1)}, bf16[16,2,160,1536]{3,2,1,0:T(8,128)(2,1)}, bf16[3,768,1536]{2,1,0:T(8,128)(2,1)}, bf16[2,2,768,1536]{3,2,1,0:T(8,128)(2,1)}) custom-call(bf16[384,2560]{1,0:T(8,128)(2,1)S(1)} %copy-done.4, bf16[384,5120]{1,0:T(8,128)(2,1)S(1)} %copy-done.2, f32[1,5120]{1,0:T(1,128)S(1)} %bitcast.10, ...), custom_call_target="tpu_custom_call" | custom-call | tf_op jit(solution)/shard_map/pallas_call | solution.py:341
  430.8 0.0 copy-start
  430.8 3.7 copy-done
  434.4 0.0 copy-start.1
  434.4 3.0 copy-done.1
  437.5 29.2 %shard_map.104 = bf16[768,1536]{1,0:T(8,128)(2,1)S(1)} custom-call(s32[3,9]{1,0:T(4,128)S(1)} %pad_dynamic-slice_fusion.mask_ref, bf16[3,768,1536]{2,1,0:T(8,128)(2,1)S(1)} %copy-done.1, bf16[3,768,1536]{2,1,0:T(8,128)(2,1)S(1)} %copy-done.1, bf16[2,2,768,1536]{3,2,1,0:T(8,128)(2,1)S(1)} %copy-done, bf16[2,2,768,1536]{3,2,1,0:T(8,128)(2,1)S(1)} %copy-done), custom_call_target="tpu_custom_call" | custom-call | tf_op jit(solution)/shard_map/pallas_call | solution.py:419
  466.7 17.7 %convolution_convert_fusion = bf16[768,5120]{1,0:T(8,128)(2,1)} fusion(bf16[768,1536]{1,0:T(8,128)(2,1)S(1)} %shard_map.104, bf16[5120,1536]{1,0:T(8,128)(2,1)} %bitcast.15), kind=kOutput, calls=%fused_computation | convolution fusion | flops 12083527680 | bytes 25952256 | tf_op jit(solution)/shard_map/dot_general | solution.py:450
  484.4 0.0 reduce-scatter.2.cloned.1.call-update
  484.5 105.5 %reduce-scatter.2.cloned.1.call-done = bf16[768,2560]{1,0:T(8,128)(2,1)} async-done(((bf16[768,5120]{1,0:T(8,128)(2,1)}), bf16[768,2560]{1,0:T(8,128)(2,1)}) %reduce-scatter.2.cloned.1.call-update) | async-done | bytes 3932176 | tf_op jit(solution)/shard_map/reduce_scatter | solution.py:453
  590.0 0.0 copy-start.3
  590.0 3.3 convert_element_type.20
  593.3 0.0 copy-done.3
  593.4 2.2 multiply_reduce_fusion
  595.5 5.5 psum.7
  601.0 2.9 slice.15
Async XLA Ops:
  7.2 582.8 %reduce-scatter.2.cloned.1.call-start = ((), (), s32[]{:S(2)}) async-start(), calls=%async_computation.1 | async-start | bytes 11796480 | tf_op jit(solution)/shard_map/reduce_scatter | solution.py:453
  8.0 4.5 copy-start.2
  8.0 5.3 copy-start.4
  8.0 5.3 copy-start.5
  430.8 3.7 copy-start
  434.4 3.0 copy-start.1
  590.0 3.3 copy-start.3
Sparse Core Ops, SparseCore 0:
  484.6 105.3 reduce-scatter.1
